TPU v7x, 128 devices: a whole 4x4x4 slice. The times are simulated.
128 devices in a mesh: row: 16 (over y, z), col: 8 (over x, core).
Axes of the slice: x: 4, y: 4, z: 4, core: 2. Of those that a mesh axis runs over, the one named last changes fastest.
Arguments:
- tokens: bfloat16 [2048, 4096], P('row', 'col'), may hold values from -6 to 6
- w_in: bfloat16 [4096, 16384], P('col', 'row'), may hold values from -0.09375 to 0.09375
- w_out: bfloat16 [16384, 4096], P('row', 'col'), may hold values from -0.046875 to 0.046875
- cotangent: bfloat16 [2048, 4096], P('row', 'col'), may hold values from -6 to 6
Outputs:
- block_out: bfloat16 [2048, 4096], P(('row', 'col'))
- grad_tokens: bfloat16 [2048, 4096], P('row', 'col')
- grad_in: float32 [4096, 16384], P('col', 'row')
- grad_out: float32 [16384, 4096], P('row', 'col')
All inputs are finite; a program needn't handle non-finite values.
Results may differ from a plain program's by a relative error of at most 0.015.
Values may be sent and summed in bfloat16 or wider, within the bound.
A program may use at most 128 MiB of HBM per device.

v0:
```python
import jax
import jax.numpy as jnp
from jax import lax
from jax.sharding import PartitionSpec as P


def gelu_grad(value):
    cdf = 0.5 * (1.0 + jax.scipy.special.erf(value * 0.7071067811865476))
    pdf = jnp.exp(-0.5 * value * value) * 0.3989422804014327
    return cdf + value * pdf


def token_panel(local_rows):
    return lax.all_gather(local_rows, "row", axis=0, tiled=True)


def hidden_panel(local_rows):
    return lax.all_gather(local_rows, "col", axis=0, tiled=True)


def contract_last(left, right):
    return lax.dot_general(
        left, right, (((1,), (1,)), ((), ())), preferred_element_type=jnp.float32
    )


def width_split(left_all, right, transposed):

    def width_term():
        if transposed:
            return contract_last(left_all, right)
        return jnp.dot(left_all, right, preferred_element_type=jnp.float32)

    return lax.psum_scatter(
        width_term().astype(jnp.bfloat16), "col", scatter_dimension=0, tiled=True
    ).astype(jnp.float32)


def unit_sum(left_all, right, transposed):

    def unit_term():
        if transposed:
            return contract_last(left_all, right)
        return jnp.dot(left_all, right, preferred_element_type=jnp.float32)

    return lax.psum_scatter(
        unit_term().astype(jnp.bfloat16), "row", scatter_dimension=0, tiled=True
    ).astype(jnp.float32)


def local(tokens, w_in, w_out, cotangent):
    tokens_all = token_panel(tokens)
    upstream_all = token_panel(cotangent)
    pre_part = width_split(tokens_all, w_in, False)
    act_all = hidden_panel(jax.nn.gelu(pre_part, approximate=False).astype(jnp.bfloat16))
    dact_part = width_split(upstream_all, w_out, True)
    dpre_all = hidden_panel((dact_part * gelu_grad(pre_part)).astype(jnp.bfloat16))
    mixed = unit_sum(act_all, w_out, False)
    block_rows = (tokens.astype(jnp.float32) + mixed).astype(jnp.bfloat16)
    block_out = lax.all_to_all(block_rows, "col", split_axis=0, concat_axis=1, tiled=True)
    grad_out = lax.dot_general(
        act_all, upstream_all, (((0,), (0,)), ((), ())), preferred_element_type=jnp.float32
    )
    grad_in = lax.dot_general(
        tokens_all, dpre_all, (((0,), (0,)), ((), ())), preferred_element_type=jnp.float32
    )
    back = unit_sum(dpre_all, w_in, True)
    grad_tokens = (cotangent.astype(jnp.float32) + back).astype(jnp.bfloat16)
    return (block_out, grad_tokens, grad_in, grad_out)


def solution(mesh):
    in_specs = (P("row", "col"), P("col", "row"), P("row", "col"), P("row", "col"))
    out_specs = (P(("row", "col"), None), P("row", "col"), P("col", "row"), P("row", "col"))
    return jax.shard_map(local, mesh=mesh, in_specs=in_specs, out_specs=out_specs, check_vma=False)
```

profile of v0, /device:TPU:0, one launch (start us, length us, event | category | flops | bytes accessed | tf_op | source)
XLA Modules:
  0.0 417.5 jit_solution(6592428128549312227)
XLA Ops:
  7.2 0.0 all-gather.9.cloned.1.call-start
  7.2 0.7 all-gather.9.cloned.1.call-update
  7.9 0.0 all-gather.5.cloned.1.call-start
  8.0 0.7 all-gather.5.cloned.1.call-update
  8.7 0.0 reduce-scatter.9.cloned.1.call-start
  8.7 49.2 %all-gather.9.cloned.1.call-done = bf16[2048,512]{1,0:T(8,128)(2,1)} async-done(((bf16[128,512]{1,0:T(8,128)(2,1)}), bf16[2048,512]{1,0:T(8,128)(2,1)}) %all-gather.9.cloned.1.call-update) | async-done | bytes 2097168 | tf_op jit(solution)/shard_map/all_gather | solution.py:14
  58.0 5.9 %convolution_convert_fusion = bf16[2048,1024]{1,0:T(8,128)(2,1)} fusion(bf16[2048,512]{1,0:T(8,128)(2,1)} %all-gather.9.cloned.1.call-done, bf16[1024,512]{1,0:T(8,128)(2,1)S(1)} %copy-done), kind=kOutput, calls=%fused_computation | convolution fusion | flops 2149580800 | bytes 7340032 | tf_op jit(solution)/shard_map/dot_general | solution.py:22
  63.9 0.0 reduce-scatter.9.cloned.1.call-update
  63.9 0.0 reduce-scatter.5.cloned.1.call-start
  64.0 40.7 %all-gather.5.cloned.1.call-done = bf16[2048,512]{1,0:T(8,128)(2,1)} async-done(((bf16[128,512]{1,0:T(8,128)(2,1)}), bf16[2048,512]{1,0:T(8,128)(2,1)}) %all-gather.5.cloned.1.call-update) | async-done | bytes 2097168 | tf_op jit(solution)/shard_map/all_gather | solution.py:14
  104.7 5.9 %convolution_convert_fusion.1 = bf16[2048,1024]{1,0:T(8,128)(2,1)} fusion(bf16[2048,512]{1,0:T(8,128)(2,1)} %all-gather.5.cloned.1.call-done, bf16[512,1024]{1,0:T(8,128)(2,1)S(1)} %copy-done.3), kind=kOutput, calls=%fused_computation.1 | convolution fusion | flops 2149580800 | bytes 7340032 | tf_op jit(solution)/shard_map/dot_general | solution.py:32
  110.6 0.0 all-gather.7.cloned.1.call-start
  110.7 33.6 %reduce-scatter.9.cloned.1.call-done = bf16[256,1024]{1,0:T(8,128)(2,1)} async-done(((bf16[2048,1024]{1,0:T(8,128)(2,1)}), bf16[256,1024]{1,0:T(8,128)(2,1)}) %reduce-scatter.9.cloned.1.call-update) | async-done | bytes 524304 | tf_op jit(solution)/shard_map/reduce_scatter | solution.py:34
  144.2 38.9 %reduce-scatter.5.cloned.1.call-done = bf16[256,1024]{1,0:T(8,128)(2,1)} async-done(((bf16[2048,1024]{1,0:T(8,128)(2,1)}), bf16[256,1024]{1,0:T(8,128)(2,1)}) %reduce-scatter.5.cloned.1.call-update) | async-done | bytes 524304 | tf_op jit(solution)/shard_map/reduce_scatter | solution.py:34
  183.2 4.6 %fusion.38 = (bf16[256,1024]{1,0:T(8,128)(2,1)}, bf16[256,1024]{1,0:T(8,128)(2,1)}) fusion(bf16[256,1024]{1,0:T(8,128)(2,1)} %reduce-scatter.5.cloned.1.call-done, bf16[256,1024]{1,0:T(8,128)(2,1)} %reduce-scatter.9.cloned.1.call-done), kind=kLoop, calls=%fused_computation.50 | loop fusion | flops 20185088 | bytes 2097152 | tf_op jit(solution)/shard_map/convert_element_type | solution.py:57
  187.8 0.0 all-gather.11.cloned.1.call-start
  187.8 0.5 all-gather.11.cloned.1.call-update
  188.3 0.0 reduce-scatter.7.cloned.1.call-start
  188.4 30.6 %all-gather.7.cloned.1.call-done = bf16[2048,1024]{1,0:T(8,128)(2,1)} async-done(((bf16[256,1024]{1,0:T(8,128)(2,1)}), bf16[2048,1024]{1,0:T(8,128)(2,1)}) %all-gather.7.cloned.1.call-update) | async-done | bytes 4194320 | tf_op jit(solution)/shard_map/all_gather | solution.py:18
  219.0 5.9 %convolution_convert_fusion.3 = bf16[2048,512]{1,0:T(8,128)(2,1)} fusion(bf16[2048,1024]{1,0:T(8,128)(2,1)} %all-gather.7.cloned.1.call-done, bf16[1024,512]{1,0:T(8,128)(2,1)S(1)} %copy-done), kind=kOutput, calls=%fused_computation.3 | convolution fusion | flops 2148532224 | bytes 7340032 | tf_op jit(solution)/shard_map/dot_general | solution.py:44
  224.9 0.2 reduce-scatter.11.cloned.1.call-start
  225.2 28.1 %all-gather.11.cloned.1.call-done = bf16[2048,1024]{1,0:T(8,128)(2,1)} async-done(((bf16[256,1024]{1,0:T(8,128)(2,1)}), bf16[2048,1024]{1,0:T(8,128)(2,1)}) %all-gather.11.cloned.1.call-update) | async-done | bytes 4194320 | tf_op jit(solution)/shard_map/all_gather | solution.py:18
  253.2 5.9 %convolution_convert_fusion.2 = bf16[2048,512]{1,0:T(8,128)(2,1)} fusion(bf16[2048,1024]{1,0:T(8,128)(2,1)} %all-gather.11.cloned.1.call-done, bf16[512,1024]{1,0:T(8,128)(2,1)S(1)} %copy-done.3), kind=kOutput, calls=%fused_computation.2 | convolution fusion | flops 2148532224 | bytes 7340032 | tf_op jit(solution)/shard_map/dot_general | solution.py:22
  259.1 5.2 %convolution_bitcast_fusion = f32[512,1024]{0,1:T(8,128)S(1)} fusion(bf16[2048,1024]{1,0:T(8,128)(2,1)} %all-gather.11.cloned.1.call-done, bf16[2048,512]{1,0:T(8,128)(2,1)} %all-gather.5.cloned.1.call-done), kind=kOutput, calls=%fused_computation.10 | convolution fusion | flops 2147483648 | bytes 8388608 | tf_op jit(solution)/shard_map/dot_general | solution.py:64
  264.4 1.8 copy.9
  266.2 6.6 %fusion.39 = f32[1024,512]{1,0:T(8,128)} fusion(bf16[2048,1024]{1,0:T(8,128)(2,1)} %all-gather.7.cloned.1.call-done, bf16[2048,512]{1,0:T(8,128)(2,1)} %all-gather.9.cloned.1.call-done), kind=kOutput, calls=%fused_computation.53 | convolution fusion | flops 2147483648 | bytes 8388608 | tf_op jit(solution)/shard_map/dot_general | solution.py:61
  272.8 58.3 %reduce-scatter.7.cloned.1.call-done = bf16[128,512]{1,0:T(8,128)(2,1)} async-done(((bf16[2048,512]{1,0:T(8,128)(2,1)}), bf16[128,512]{1,0:T(8,128)(2,1)}) %reduce-scatter.7.cloned.1.call-update) | async-done | bytes 131088 | tf_op jit(solution)/shard_map/reduce_scatter | solution.py:46
  331.1 1.6 add_convert_fusion.1
  332.6 4.2 %all-to-all-start = ((bf16[8,16,512]{2,1,0:T(8,128)(2,1)}), bf16[8,16,512]{2,1,0:T(8,128)(2,1)S(1)}, u32[]{:S(2)}, u32[]{:S(2)}) async-start(bf16[8,16,512]{2,1,0:T(8,128)(2,1)} %bitcast), calls=%async_computation.2 | async-start | bytes 262144 | tf_op jit(solution)/shard_map/all_to_all | solution.py:60
  336.9 71.5 %reduce-scatter.11.cloned.1.call-done = bf16[128,512]{1,0:T(8,128)(2,1)} async-done(((bf16[2048,512]{1,0:T(8,128)(2,1)}), bf16[128,512]{1,0:T(8,128)(2,1)}) %reduce-scatter.11.cloned.1.call-update) | async-done | bytes 131088 | tf_op jit(solution)/shard_map/reduce_scatter | solution.py:46
  408.4 1.6 add_convert_fusion
  410.0 0.7 copy.10
  (13 shorter events, 0.1 us)
Async XLA Ops:
  7.2 50.8 %copy-start = (bf16[1024,512]{1,0:T(8,128)(2,1)S(1)}, bf16[1024,512]{1,0:T(8,128)(2,1)}, u32[]{:S(2)}) copy-start(bf16[1024,512]{1,0:T(8,128)(2,1)} %param.6) | copy-start | bytes 3145732
  7.2 50.8 %all-gather.9.cloned.1.call-start = ((), (), s32[]{:S(2)}) async-start(), calls=%async_computation.9 | async-start | bytes 2228224 | tf_op jit(solution)/shard_map/all_gather | solution.py:14
  7.9 96.7 %all-gather.5.cloned.1.call-start = ((), (), s32[]{:S(2)}) async-start(), calls=%async_computation.5 | async-start | bytes 2228224 | tf_op jit(solution)/shard_map/all_gather | solution.py:14
  8.7 135.6 %reduce-scatter.9.cloned.1.call-start = ((), (), s32[]{:S(2)}) async-start(), calls=%async_computation.10 | async-start | bytes 4718592 | tf_op jit(solution)/shard_map/reduce_scatter | solution.py:34
  63.9 40.8 %copy-start.3 = (bf16[512,1024]{1,0:T(8,128)(2,1)S(1)}, bf16[512,1024]{1,0:T(8,128)(2,1)}, u32[]{:S(2)}) copy-start(bf16[512,1024]{1,0:T(8,128)(2,1)} %param.5) | copy-start | bytes 3145732
  63.9 119.3 %reduce-scatter.5.cloned.1.call-start = ((), (), s32[]{:S(2)}) async-start(), calls=%async_computation.6 | async-start | bytes 4718592 | tf_op jit(solution)/shard_map/reduce_scatter | solution.py:34
  110.6 108.4 %all-gather.7.cloned.1.call-start = ((), (), s32[]{:S(2)}) async-start(), calls=%async_computation.7 | async-start | bytes 4718592 | tf_op jit(solution)/shard_map/all_gather | solution.py:18
  187.8 65.5 %all-gather.11.cloned.1.call-start = ((), (), s32[]{:S(2)}) async-start(), calls=%async_computation.11 | async-start | bytes 4718592 | tf_op jit(solution)/shard_map/all_gather | solution.py:18
  188.3 142.7 %reduce-scatter.7.cloned.1.call-start = ((), (), s32[]{:S(2)}) async-start(), calls=%async_computation.8 | async-start | bytes 2228224 | tf_op jit(solution)/shard_map/reduce_scatter | solution.py:46
  224.9 183.5 %reduce-scatter.11.cloned.1.call-start = ((), (), s32[]{:S(2)}) async-start(), calls=%async_computation.12 | async-start | bytes 2228224 | tf_op jit(solution)/shard_map/reduce_scatter | solution.py:46
  266.2 64.9 %copy-start.1 = (bf16[128,512]{1,0:T(8,128)(2,1)S(1)}, bf16[128,512]{1,0:T(8,128)(2,1)}, u32[]{:S(2)}) copy-start(bf16[128,512]{1,0:T(8,128)(2,1)} %param.4) | copy-start | bytes 393220
  266.2 142.2 %copy-start.2 = (bf16[128,512]{1,0:T(8,128)(2,1)S(1)}, bf16[128,512]{1,0:T(8,128)(2,1)}, u32[]{:S(2)}) copy-start(bf16[128,512]{1,0:T(8,128)(2,1)} %param.7) | copy-start | bytes 393220
  332.6 77.4 %all-to-all-start = ((bf16[8,16,512]{2,1,0:T(8,128)(2,1)}), bf16[8,16,512]{2,1,0:T(8,128)(2,1)S(1)}, u32[]{:S(2)}, u32[]{:S(2)}) async-start(bf16[8,16,512]{2,1,0:T(8,128)(2,1)} %bitcast), calls=%async_computation.2 | async-start | bytes 262144 | tf_op jit(solution)/shard_map/all_to_all | solution.py:60
Sparse Core Ops, SparseCore 0:
  10.2 47.7 all-gather.8
  60.1 44.5 all-gather.4
  107.1 37.1 reduce-scatter.8
  146.5 36.6 reduce-scatter.4
  187.9 31.0 all-gather.6
  221.2 32.0 all-gather.10
  256.5 74.5 reduce-scatter.6
  334.7 73.7 reduce-scatter.10
where the time goes:
time: 418 us
  waiting for transfers between devices  353 us (84%)
  matrix products  35.4 us (8%)
  between operations  14.2 us (3%)
  other arithmetic  7.74 us (2%)
  starting transfers between devices  4.75 us (1%)
    reduce_scatter x2, waiting for transfers between devices, unit_sum(): lax.psum_scatter(unit_term().astype(jnp.bfloat16), 'row', scatter_dimensi...  130 us
    all_gather x2, waiting for transfers between devices, token_panel(): return lax.all_gather(local_rows, 'row', axis=0, tiled=True)  89.9 us
    reduce_scatter x2, waiting for transfers between devices, width_split(): lax.psum_scatter(width_term().astype(jnp.bfloat16), 'col', scatter_dimens...  72.5 us
    all_gather x2, waiting for transfers between devices, hidden_panel(): return lax.all_gather(local_rows, 'col', axis=0, tiled=True)  58.7 us
    dot_general x2, matrix products, contract_last(): lax.dot_general(left, right, (((1,), (1,)), ((), ())), preferred_element_...  11.8 us
  transfers between devices with their start and end apart: 9, of which 8 were waited for; matrix products, arithmetic and copies ran while one was open for 10% of the time, Pallas kernels for 0%

commit v1 on v0

--- a/solution.py
+++ b/solution.py
@@ -11,7 +11,9 @@
 
 
 def token_panel(local_rows):
-    return lax.all_gather(local_rows, "row", axis=0, tiled=True)
+    return jnp.concatenate(
+        lax.all_to_all(jnp.stack([local_rows] * lax.axis_size("row")), "row", 0, 0), axis=0
+    )
 
 
 def hidden_panel(local_rows):

time: 418 us -> 359 us (0.86)
  waiting for transfers between devices: 353 us -> 225 us
  blocking collectives: 0 us -> 67.2 us
  local copies, waits for them, and re-layouts: 2.5 us -> 7.09 us
    all_gather x2 -> x0, waiting for transfers between devices: 89.9 us -> none  [token_panel(): return lax.all_gather(local_rows, 'row', axis=0, tiled=True)]
    all_to_all x0 -> x2, blocking collectives: none -> 67.2 us  [token_panel(): lax.all_to_all(jnp.stack([local_rows] * lax.axis_size('row')), 'row', 0, 0)]
    reduce_scatter x2, waiting for transfers between devices: 72.5 us -> 38 us  [width_split(): lax.psum_scatter(width_term().astype(jnp.bfloat16), 'col', scatter_dimens...]
  transfers between devices with their start and end apart: 9 -> 7, of which waited for: 8 -> 5; matrix products, arithmetic and copies ran while one was open for 10% -> 10% of each run, Pallas kernels for 0% -> 0%
where the time goes in v1:
time: 359 us
  waiting for transfers between devices  225 us (63%)
  blocking collectives  67.2 us (19%)
  matrix products  33.2 us (9%)
  between operations  14.2 us (4%)
  other arithmetic  7.74 us (2%)
  local copies, waits for them, and re-layouts  7.09 us (2%)
  starting transfers between devices  4.67 us (1%)
    reduce_scatter x2, waiting for transfers between devices, unit_sum(): lax.psum_scatter(unit_term().astype(jnp.bfloat16), 'row', scatter_dimensi...  128 us
    all_to_all x2, blocking collectives, token_panel(): lax.all_to_all(jnp.stack([local_rows] * lax.axis_size('row')), 'row', 0, 0)  67.2 us
    all_gather x2, waiting for transfers between devices, hidden_panel(): return lax.all_gather(local_rows, 'col', axis=0, tiled=True)  58.6 us
    reduce_scatter x2, waiting for transfers between devices, width_split(): lax.psum_scatter(width_term().astype(jnp.bfloat16), 'col', scatter_dimens...  38 us
    dot_general x2, matrix products, contract_last(): lax.dot_general(left, right, (((1,), (1,)), ((), ())), preferred_element_...  10.5 us
  transfers between devices with their start and end apart: 7, of which 5 were waited for; matrix products, arithmetic and copies ran while one was open for 10% of the time, Pallas kernels for 0%

profile of v1, /device:TPU:0, one launch (start us, length us, event | category | flops | bytes accessed | tf_op | source)
XLA Modules:
  0.0 358.7 jit_solution(18397980137955862737)
XLA Ops:
  7.2 0.0 reduce-scatter.9.cloned.1.call-start
  7.2 1.2 stack.5
  8.4 36.2 %all_to_all.29 = bf16[16,128,512]{2,1,0:T(8,128)(2,1)S(1)} all-to-all(bf16[16,128,512]{2,1,0:T(8,128)(2,1)S(1)} %stack.5), channel_id=1, replica_groups=mesh['row'=16,'col'=8] {'row'}, dimensions={0} | all-to-all | bytes 4194304 | tf_op jit(solution)/shard_map/all_to_all | solution.py:15
  44.6 4.3 %convolution_convert_fusion = bf16[2048,1024]{1,0:T(8,128)(2,1)} fusion(bf16[2048,512]{1,0:T(8,128)(2,1)S(1)} %bitcast.20, bf16[1024,512]{1,0:T(8,128)(2,1)S(1)} %copy-done), kind=kOutput, calls=%fused_computation | convolution fusion | flops 2149580800 | bytes 7340032 | tf_op jit(solution)/shard_map/dot_general | solution.py:24
  48.9 0.0 reduce-scatter.5.cloned.1.call-start
  49.0 0.8 copy-done.2
  49.8 0.2 stack.4
  50.0 31.0 %all_to_all.30 = bf16[16,128,512]{2,1,0:T(8,128)(2,1)S(1)} all-to-all(bf16[16,128,512]{2,1,0:T(8,128)(2,1)S(1)} %stack.4), channel_id=1, replica_groups=mesh['row'=16,'col'=8] {'row'}, dimensions={0} | all-to-all | bytes 4194304 | tf_op jit(solution)/shard_map/all_to_all | solution.py:15
  81.0 1.3 copy-done.1
  82.3 4.3 %convolution_convert_fusion.1 = bf16[2048,1024]{1,0:T(8,128)(2,1)} fusion(bf16[2048,512]{1,0:T(8,128)(2,1)S(1)} %bitcast.22, bf16[512,1024]{1,0:T(8,128)(2,1)S(1)} %copy-done.4), kind=kOutput, calls=%fused_computation.1 | convolution fusion | flops 2149580800 | bytes 7340032 | tf_op jit(solution)/shard_map/dot_general | solution.py:34
  86.7 0.0 reduce-scatter.5.cloned.1.call-update
  86.7 0.0 all-gather.3.cloned.1.call-start
  86.7 0.0 reduce-scatter.9.cloned.1.call-done
  86.8 38.0 %reduce-scatter.5.cloned.1.call-done = bf16[256,1024]{1,0:T(8,128)(2,1)} async-done(((bf16[2048,1024]{1,0:T(8,128)(2,1)}), bf16[256,1024]{1,0:T(8,128)(2,1)}) %reduce-scatter.5.cloned.1.call-update) | async-done | bytes 524304 | tf_op jit(solution)/shard_map/reduce_scatter | solution.py:36
  124.7 4.6 %fusion.38 = (bf16[256,1024]{1,0:T(8,128)(2,1)}, bf16[256,1024]{1,0:T(8,128)(2,1)}) fusion(bf16[256,1024]{1,0:T(8,128)(2,1)} %reduce-scatter.5.cloned.1.call-done, bf16[256,1024]{1,0:T(8,128)(2,1)} %reduce-scatter.9.cloned.1.call-done), kind=kLoop, calls=%fused_computation.50 | loop fusion | flops 20185088 | bytes 2097152 | tf_op jit(solution)/shard_map/convert_element_type | solution.py:59
  129.3 0.0 all-gather.5.cloned.1.call-start
  129.4 0.5 all-gather.5.cloned.1.call-update
  129.9 0.0 reduce-scatter.7.cloned.1.call-start
  129.9 30.5 %all-gather.3.cloned.1.call-done = bf16[2048,1024]{1,0:T(8,128)(2,1)} async-done(((bf16[256,1024]{1,0:T(8,128)(2,1)}), bf16[2048,1024]{1,0:T(8,128)(2,1)}) %all-gather.3.cloned.1.call-update) | async-done | bytes 4194320 | tf_op jit(solution)/shard_map/all_gather | solution.py:20
  160.4 5.9 %convolution_convert_fusion.3 = bf16[2048,512]{1,0:T(8,128)(2,1)} fusion(bf16[2048,1024]{1,0:T(8,128)(2,1)} %all-gather.3.cloned.1.call-done, bf16[1024,512]{1,0:T(8,128)(2,1)S(1)} %copy-done), kind=kOutput, calls=%fused_computation.3 | convolution fusion | flops 2148532224 | bytes 7340032 | tf_op jit(solution)/shard_map/dot_general | solution.py:46
  166.4 0.2 reduce-scatter.11.cloned.1.call-start
  166.6 28.1 %all-gather.5.cloned.1.call-done = bf16[2048,1024]{1,0:T(8,128)(2,1)} async-done(((bf16[256,1024]{1,0:T(8,128)(2,1)}), bf16[2048,1024]{1,0:T(8,128)(2,1)}) %all-gather.5.cloned.1.call-update) | async-done | bytes 4194320 | tf_op jit(solution)/shard_map/all_gather | solution.py:20
  194.7 6.2 %convolution_convert_fusion.2 = bf16[2048,512]{1,0:T(8,128)(2,1)} fusion(bf16[2048,1024]{1,0:T(8,128)(2,1)} %all-gather.5.cloned.1.call-done, bf16[512,1024]{1,0:T(8,128)(2,1)} %param.5), kind=kOutput, calls=%fused_computation.2 | convolution fusion | flops 2148532224 | bytes 7340032 | tf_op jit(solution)/shard_map/dot_general | solution.py:24
  200.9 6.6 %convolution_bitcast_fusion = f32[512,1024]{0,1:T(8,128)} fusion(bf16[2048,1024]{1,0:T(8,128)(2,1)} %all-gather.5.cloned.1.call-done, bf16[2048,512]{1,0:T(8,128)(2,1)} %bitcast.23), kind=kOutput, calls=%fused_computation.10 | convolution fusion | flops 2147483648 | bytes 8388608 | tf_op jit(solution)/shard_map/dot_general | solution.py:66
  207.4 2.9 copy.9
  210.3 5.9 %fusion.39 = f32[1024,512]{1,0:T(8,128)} fusion(bf16[2048,1024]{1,0:T(8,128)(2,1)} %all-gather.3.cloned.1.call-done, bf16[2048,512]{1,0:T(8,128)(2,1)S(1)} %bitcast.21), kind=kOutput, calls=%fused_computation.53 | convolution fusion | flops 2147483648 | bytes 8388608 | tf_op jit(solution)/shard_map/dot_general | solution.py:63
  216.2 56.1 %reduce-scatter.7.cloned.1.call-done = bf16[128,512]{1,0:T(8,128)(2,1)} async-done(((bf16[2048,512]{1,0:T(8,128)(2,1)}), bf16[128,512]{1,0:T(8,128)(2,1)}) %reduce-scatter.7.cloned.1.call-update) | async-done | bytes 131088 | tf_op jit(solution)/shard_map/reduce_scatter | solution.py:48
  272.4 1.6 add_convert_fusion.1
  274.0 4.2 %all-to-all-start.1 = ((bf16[8,16,512]{2,1,0:T(8,128)(2,1)}), bf16[8,16,512]{2,1,0:T(8,128)(2,1)S(1)}, u32[]{:S(2)}, u32[]{:S(2)}) async-start(bf16[8,16,512]{2,1,0:T(8,128)(2,1)} %bitcast.1), calls=%async_computation.3 | async-start | bytes 262144 | tf_op jit(solution)/shard_map/all_to_all | solution.py:62
  278.2 71.4 %reduce-scatter.11.cloned.1.call-done = bf16[128,512]{1,0:T(8,128)(2,1)} async-done(((bf16[2048,512]{1,0:T(8,128)(2,1)}), bf16[128,512]{1,0:T(8,128)(2,1)}) %reduce-scatter.11.cloned.1.call-update) | async-done | bytes 131088 | tf_op jit(solution)/shard_map/reduce_scatter | solution.py:48
  349.6 1.6 add_convert_fusion
  351.2 0.7 copy.10
  (13 shorter events, 0.1 us)
Async XLA Ops:
  7.2 37.4 %copy-start = (bf16[1024,512]{1,0:T(8,128)(2,1)S(1)}, bf16[1024,512]{1,0:T(8,128)(2,1)}, u32[]{:S(2)}) copy-start(bf16[1024,512]{1,0:T(8,128)(2,1)} %param.6) | copy-start | bytes 3145732
  7.2 79.6 %reduce-scatter.9.cloned.1.call-start = ((), (), s32[]{:S(2)}) async-start(), calls=%async_computation.10 | async-start | bytes 4718592 | tf_op jit(solution)/shard_map/reduce_scatter | solution.py:36
  48.9 0.9 copy-start.2
  48.9 75.8 %reduce-scatter.5.cloned.1.call-start = ((), (), s32[]{:S(2)}) async-start(), calls=%async_computation.7 | async-start | bytes 4718592 | tf_op jit(solution)/shard_map/reduce_scatter | solution.py:36
  50.0 32.3 %copy-start.4 = (bf16[512,1024]{1,0:T(8,128)(2,1)S(1)}, bf16[512,1024]{1,0:T(8,128)(2,1)}, u32[]{:S(2)}) copy-start(bf16[512,1024]{1,0:T(8,128)(2,1)} %param.5) | copy-start | bytes 3145732
  81.0 1.3 copy-start.1
  86.7 73.8 %all-gather.3.cloned.1.call-start = ((), (), s32[]{:S(2)}) async-start(), calls=%async_computation.8 | async-start | bytes 4718592 | tf_op jit(solution)/shard_map/all_gather | solution.py:20
  129.3 65.4 %all-gather.5.cloned.1.call-start = ((), (), s32[]{:S(2)}) async-start(), calls=%async_computation.11 | async-start | bytes 4718592 | tf_op jit(solution)/shard_map/all_gather | solution.py:20
  129.9 142.5 %reduce-scatter.7.cloned.1.call-start = ((), (), s32[]{:S(2)}) async-start(), calls=%async_computation.9 | async-start | bytes 2228224 | tf_op jit(solution)/shard_map/reduce_scatter | solution.py:48
  166.4 183.2 %reduce-scatter.11.cloned.1.call-start = ((), (), s32[]{:S(2)}) async-start(), calls=%async_computation.12 | async-start | bytes 2228224 | tf_op jit(solution)/shard_map/reduce_scatter | solution.py:48
  210.3 139.3 %copy-start.3 = (bf16[128,512]{1,0:T(8,128)(2,1)S(1)}, bf16[128,512]{1,0:T(8,128)(2,1)}, u32[]{:S(2)}) copy-start(bf16[128,512]{1,0:T(8,128)(2,1)} %param.7) | copy-start | bytes 393220
  274.0 77.2 %all-to-all-start.1 = ((bf16[8,16,512]{2,1,0:T(8,128)(2,1)}), bf16[8,16,512]{2,1,0:T(8,128)(2,1)S(1)}, u32[]{:S(2)}, u32[]{:S(2)}) async-start(bf16[8,16,512]{2,1,0:T(8,128)(2,1)} %bitcast.1), calls=%async_computation.3 | async-start | bytes 262144 | tf_op jit(solution)/shard_map/all_to_all | solution.py:62
Sparse Core Ops, SparseCore 0:
  49.1 36.7 reduce-scatter.8
  88.2 36.4 reduce-scatter.4
  129.4 30.9 all-gather.2
  162.6 32.0 all-gather.4
  197.8 74.5 reduce-scatter.6
  275.9 73.7 reduce-scatter.10
